TPU v7x, 32 devices: a whole 2x2x4 slice. The times are simulated.
32 devices in a mesh: gx: 8 (over z, x), gy: 2 (over y), gz: 2 (over core).
Axes of the slice: x: 2, y: 2, z: 4, core: 2. Of those that a mesh axis runs over, the one named last changes fastest.
Arguments:
- state_field: float32 [128, 5, 32, 256], P('gx', None, 'gy', 'gz'), may hold values from -6 to 6
- source: float32 [128, 5, 32, 256], P('gx', None, 'gy', 'gz'), may hold values from -6 to 6
- fluid_mask: int32 [128, 32, 256], P('gx', 'gy', 'gz'), may hold values 0 or 1
- cell_kind: int32 [128, 32, 256], P('gx', 'gy', 'gz'), may hold values from 0 to 2
- boundary_side_number: int32 [128, 32, 256], P('gx', 'gy', 'gz'), may hold values from 0 to 11
- center_matrix: float32 [5, 5], replicated, may hold values from -2.5 to 2.5
- flux_jacobian_blocks: float32 [6, 5, 5], replicated, may hold values from -1 to 1
- wall_matrix: float32 [5, 5], replicated, may hold values from -2.5 to 2.5
- diag_inverse: float32 [128, 5, 5, 32, 256], P('gx', None, None, 'gy', 'gz'), may hold values from -0.01 to 0.1
- lower_coupling: float32 [5, 5], replicated, may hold values from -10 to 10
- upper_neighbour_block: float32 [5, 5], replicated, may hold values from -10 to 10
Outputs:
- update: float32 [128, 5, 32, 256], P('gx', None, 'gy', 'gz')
- residual: float32 [128, 5, 32, 256], P('gx', None, 'gy', 'gz')
Inputs may be any that keep to these rules, and one draw needn't show every extreme that they name: `boundary_side_number`: values 0 to 5 name the face of a cell that is a wall (lower x, upper x, lower y, upper y, lower z, upper z); 6 or more: no wall face. `cell_kind`: 0 full cell, 1 cut cell, 2 small cut cell.
All inputs are finite; a program needn't handle non-finite values. No bound on the sum of `fluid_mask` on one device may be relied on, other than what follows from the above.
Results may differ from a plain program's by a relative error of at most 0.00018.
Values sent between devices are 32-bit elements; how exact they have to be, the bound alone decides.
No kernel may reach another device: no remote copies, remote signals or barrier semaphores. Data moves between devices by JAX's collectives and lax.ppermute only.
A program may use at most 64 MiB of HBM per device.

v0:
```python
import jax
import jax.numpy as jnp
from jax import lax
from jax.sharding import PartitionSpec as P


def with_halo(block, sides, width):
    for axis, dim in sides:
        count = lax.axis_size(axis)
        forward = [(i, i + 1) for i in range(count - 1)]
        backward = [(target, source) for source, target in forward]
        low = lax.ppermute(
            lax.slice_in_dim(block, block.shape[dim] - width, None, axis=dim), axis, forward
        )
        high = lax.ppermute(lax.slice_in_dim(block, 0, width, axis=dim), axis, backward)
        block = jnp.concatenate([low, block, high], axis=dim)
    return block


def const_apply(matrix, vector):
    return jnp.einsum("ab,...byz->...ayz", matrix, vector, precision=lax.Precision.HIGHEST)


def couple(matrix, transfer):
    return jnp.einsum("ab,bcyz->acyz", matrix, transfer, precision=lax.Precision.HIGHEST)


def volume_operator(blocks, vector):
    return jnp.sum(blocks * vector[..., None, :, :, :], axis=-3)


def cell_product(left, right):
    return jnp.sum(left[:, :, None] * right[None], axis=1)


def flux_residual(
    state_field,
    padded,
    source,
    fluid,
    cell_kind,
    boundary_side_number,
    center_matrix,
    flux_jacobian_blocks,
    wall_matrix,
):
    neighbours = [
        padded[:-2, :, 1:-1, 1:-1],
        padded[2:, :, 1:-1, 1:-1],
        padded[1:-1, :, :-2, 1:-1],
        padded[1:-1, :, 2:, 1:-1],
        padded[1:-1, :, 1:-1, :-2],
        padded[1:-1, :, 1:-1, 2:],
    ]
    walled = const_apply(wall_matrix, state_field)
    flux = const_apply(center_matrix, state_field)
    for facing in range(6):
        at_wall = (boundary_side_number == facing)[:, None]
        flux = flux + jnp.where(
            at_wall, walled, const_apply(flux_jacobian_blocks[facing], neighbours[facing])
        )
    weight = jnp.where(cell_kind == 0, 1.0, jnp.where(cell_kind == 1, 2.0, 4.0)).astype(jnp.float32)
    return fluid[:, None] * (source - flux) * weight[:, None]


def pack_maps(transfer, offset):
    comps = offset.shape[0]
    columns = offset.shape[1] * offset.shape[2]
    packed = jnp.concatenate(
        [transfer.reshape(comps * comps, columns), offset.reshape(comps, columns)], axis=0
    )
    return packed[None]


def column_chain(spread, comps, backwards):
    groups = spread.shape[0]
    columns = spread.shape[2]
    matrices = spread[:, : comps * comps].reshape(groups, comps, comps, columns)
    offsets = spread[:, comps * comps :]

    def chain_step(carry, inputs):
        matrix, shift_term = inputs
        following = jnp.sum(matrix * carry[None, :, :], axis=1) + shift_term
        return (following, carry)

    start = jnp.zeros((comps, columns), jnp.float32)
    final, incoming = lax.scan(chain_step, start, (matrices, offsets), reverse=backwards)
    return incoming


def carry_east(transfer, offset):
    spread = lax.all_to_all(
        pack_maps(transfer, offset), "gx", split_axis=2, concat_axis=0, tiled=True
    )
    incoming = column_chain(spread, offset.shape[0], False)
    returned = lax.all_to_all(incoming, "gx", split_axis=0, concat_axis=2, tiled=True)
    return returned.reshape(offset.shape)


def carry_west(transfer, offset):
    spread = lax.all_to_all(
        pack_maps(transfer, offset), "gx", split_axis=2, concat_axis=0, tiled=True
    )
    incoming = column_chain(spread, offset.shape[0], True)
    returned = lax.all_to_all(incoming, "gx", split_axis=0, concat_axis=2, tiled=True)
    return returned.reshape(offset.shape)


def on_device(
    state_field,
    source,
    fluid_mask,
    cell_kind,
    boundary_side_number,
    center_matrix,
    flux_jacobian_blocks,
    wall_matrix,
    diag_inverse,
    lower_coupling,
    upper_neighbour_block,
):
    fluid = fluid_mask.astype(jnp.float32)
    masked = state_field * fluid[:, None]
    padded = with_halo(masked, (("gx", 0), ("gy", 2), ("gz", 3)), 1)
    residual = flux_residual(
        state_field,
        padded,
        source,
        fluid,
        cell_kind,
        boundary_side_number,
        center_matrix,
        flux_jacobian_blocks,
        wall_matrix,
    )
    comps = state_field.shape[1]
    plane_shape = (comps, state_field.shape[2], state_field.shape[3])
    zeroed = jnp.zeros(plane_shape, jnp.float32)
    identity = jnp.broadcast_to(
        jnp.eye(comps, dtype=jnp.float32)[:, :, None, None], (comps, comps) + plane_shape[1:]
    )

    def forward_map(carry, inputs):
        value, transfer = carry
        blocks, term = inputs
        value = volume_operator(blocks, term + const_apply(lower_coupling, value))
        transfer = cell_product(blocks, couple(lower_coupling, transfer))
        return ((value, transfer), None)

    def forward(carry, inputs):
        blocks, term = inputs
        carry = volume_operator(blocks, term + const_apply(lower_coupling, carry))
        return (carry, carry)

    (offset, transfer), unused = lax.scan(forward_map, (zeroed, identity), (diag_inverse, residual))
    incoming = carry_east(transfer, offset)
    final, swept = lax.scan(forward, incoming, (diag_inverse, residual))

    def backward_map(carry, inputs):
        value, transfer = carry
        blocks, term = inputs
        value = term - volume_operator(blocks, const_apply(upper_neighbour_block, value))
        transfer = -cell_product(blocks, couple(upper_neighbour_block, transfer))
        return ((value, transfer), None)

    def backward(carry, inputs):
        blocks, value = inputs
        carry = value - volume_operator(blocks, const_apply(upper_neighbour_block, carry))
        return (carry, carry)

    (offset, transfer), unused = lax.scan(
        backward_map, (zeroed, identity), (diag_inverse, swept), reverse=True
    )
    incoming = carry_west(transfer, offset)
    final, update = lax.scan(backward, incoming, (diag_inverse, swept), reverse=True)
    return (update, residual)


def solution(mesh):
    in_specs = (
        P("gx", None, "gy", "gz"),
        P("gx", None, "gy", "gz"),
        P("gx", "gy", "gz"),
        P("gx", "gy", "gz"),
        P("gx", "gy", "gz"),
        P(),
        P(),
        P(),
        P("gx", None, None, "gy", "gz"),
        P(),
        P(),
    )
    out_specs = (P("gx", None, "gy", "gz"), P("gx", None, "gy", "gz"))
    return jax.shard_map(
        on_device, mesh=mesh, in_specs=in_specs, out_specs=out_specs, check_vma=False
    )
```

profile of v0, /device:TPU:0, one launch (start us, length us, event | category | flops | bytes accessed | tf_op | source)
XLA Modules:
  0.0 266.1 jit_solution(13816744103888163784)
XLA Ops:
  3.2 5.0 %collective-permute-start = (f32[1,5,16,128]{3,1,2,0:T(8,128)S(1)}, f32[1,5,16,128]{3,1,2,0:T(8,128)S(1)}, u32[]{:S(2)}, u32[]{:S(2)}) collective-permute-start(f32[1,5,16,128]{3,1,2,0:T(8,128)S(1)} %get-tuple-element.649), channel_id=1, source_target_pairs={{0,4},{4,8},{8,12},{12,16},{16,20},{20,24},{24,28},{1,5},{5,9},{9,... | collective-permute-start | bytes 122888 | tf_op jit(solution)/shard_map/ppermute | solution.py:12
  11.5 2.2 fusion.37
  14.4 3.4 %collective-permute-start.2 = (f32[18,5,1,128]{3,1,2,0:T(8,128)S(1)}, f32[18,5,1,128]{3,1,2,0:T(8,128)S(1)}, u32[]{:S(2)}, u32[]{:S(2)}) collective-permute-start(f32[18,5,1,128]{3,1,2,0:T(8,128)S(1)} %get-tuple-element.647), channel_id=1, source_target_pairs={{0,2},{1,3},{4,6},{5,7},{8,10},{9,11},{12,14},{13,15},{16,18},{17,... | collective-permute-start | bytes 138248 | tf_op jit(solution)/shard_map/ppermute | solution.py:12
  21.3 2.8 %collective-permute-done.3 = f32[18,5,1,128]{3,1,2,0:T(8,128)S(1)} collective-permute-done((f32[18,5,1,128]{3,1,2,0:T(8,128)S(1)}, f32[18,5,1,128]{3,1,2,0:T(8,128)S(1)}, u32[]{:S(2)}, u32[]{:S(2)}) %collective-permute-start.3) | collective-permute-done | bytes 46112 | tf_op jit(solution)/shard_map/ppermute | solution.py:15
  26.4 2.6 copy.197
  33.6 3.0 %convolution_select_fusion = f32[16,16,128,5]{2,3,1,0:T(8,128)} fusion(f32[16,16,128,5]{2,3,1,0:T(8,128)S(1)} %fusion.35, f32[18,5,1,128]{3,1,2,0:T(8,128)} %copy-done.16, f32[1,5,16,128]{3,1,2,0:T(8,128)} %copy-done.6, f32[16,5,16,128]{3,1,2,0:T(8,128)S(1)} %copy_multiply_fusion, f32[1,5,16,128]{3,1,2,0:T(8,128)S(1)} %collective-permute-done, ...), kind=kOutput, calls=%fused_computation.52 | convolution fusion | flops 10581760 | bytes 2126948 | tf_op jit(solution)/shard_map/ab,...byz->...ayz/dot_general | solution.py:21
  38.8 2.8 %copy.198 = f32[18,5,18,1]{3,1,2,0:T(8,128)} copy(f32[18,5,18,1]{2,3,1,0:T(1,128)} %collective-permute-done.4) | data formatting | bytes 12960 | tf_op jit(solution)/shard_map/ppermute | solution.py:12
  43.4 2.6 convolution_select_fusion.5
  50.1 28.6 %while.87 = (s32[]{:T(128)}, f32[5,16,128]{2,1,0:T(8,128)S(1)}, f32[5,5,16,128]{3,2,1,0:T(8,128)S(1)}, f32[16,5,5,16,128]{4,3,2,1,0:T(8,128)}, f32[16,5,16,128]{...) while((s32[]{:T(128)}, f32[5,16,128]{2,1,0:T(8,128)S(1)}, f32[5,5,16,128]{3,2,1,0:T(8,128)S(1)}, ...), condition=%wide.region_3.4_spmd, body=%wide.region_0.3_spmd.sunk | while | flops 4249602 | bytes 2130205 | solution.py:155
  80.1 9.3 %reduce = f32[2048,30]{1,0:T(8,128)S(1)} reduce(f32[2048,1,30]{2,1,0:T(1,128)S(1)} %bitcast.220, f32[]{:T(128)} %broadcast.68), dimensions={1}, to_apply=%bitcast.170.reduce_sub_computation | reduce | bytes 491524
  91.2 7.0 %all-to-all-start = ((f32[8,1,7680]{2,1,0:T(1,128)}), f32[8,1,7680]{2,1,0:T(1,128)S(1)}, u32[]{:S(2)}, u32[]{:S(2)}) async-start(f32[8,1,7680]{2,1,0:T(1,128)} %reshape.87), calls=%async_computation | async-start | bytes 491520 | tf_op jit(solution)/shard_map/all_to_all | solution.py:92
  98.1 9.7 %all-to-all-done = f32[8,1,7680]{2,1,0:T(1,128)S(1)} async-done(((f32[8,1,7680]{2,1,0:T(1,128)}), f32[8,1,7680]{2,1,0:T(1,128)S(1)}, u32[]{:S(2)}, u32[]{:S(2)}) %all-to-all-start) | async-done | bytes 245792 | tf_op jit(solution)/shard_map/all_to_all | solution.py:92
  111.9 5.7 %while.90 = (s32[]{:T(128)}, f32[5,256]{1,0:T(8,128)S(1)}, f32[8,5,256]{2,1,0:T(8,128)}, f32[8,5,5,256]{3,0,2,1:T(8,128)S(1)}, f32[8,5,256]{2,0,1:T(8,128)S(1)}, /*index=5*/s32[]{:T(128)}, s32[]{:T(128)}) while((s32[]{:T(128)}, f32[5,256]{1,0:T(8,128)S(1)}, f32[8,5,256]{2,1,0:T(8,128)}, f32[8,5,5,256]{3,0,2,1:T(8,128)S(1)}, ...), condition=%wide.region_6.7_spmd.clone, body=%wide.region_4.6_spmd.clone.sunk | while | flops 14083 | bytes 131679 | solution.py:87
  117.6 3.9 %all-to-all-start.1 = ((f32[8,5,256]{2,1,0:T(8,128)}), f32[8,5,256]{2,1,0:T(8,128)S(1)}, u32[]{:S(2)}, u32[]{:S(2)}) async-start(f32[8,5,256]{2,1,0:T(8,128)} %get-tuple-element.444), calls=%async_computation.1 | async-start | bytes 131072 | tf_op jit(solution)/shard_map/all_to_all | solution.py:96
  121.5 6.9 %all-to-all-done.1 = f32[8,5,256]{2,1,0:T(8,128)S(1)} async-done(((f32[8,5,256]{2,1,0:T(8,128)}), f32[8,5,256]{2,1,0:T(8,128)S(1)}, u32[]{:S(2)}, u32[]{:S(2)}) %all-to-all-start.1) | async-done | bytes 40992 | tf_op jit(solution)/shard_map/all_to_all | solution.py:96
  128.5 19.3 %while.88 = (s32[]{:T(128)}, f32[5,16,128]{2,1,0:T(8,128)S(1)}, f32[16,5,16,128]{3,2,1,0:T(8,128)S(1)}, f32[16,5,5,16,128]{4,3,2,1,0:T(8,128)}, f32[16,5,16,128]...) while((s32[]{:T(128)}, f32[5,16,128]{2,1,0:T(8,128)S(1)}, f32[16,5,16,128]{3,2,1,0:T(8,128)S(1)}, ...), condition=%wide.region_9.10_spmd, body=%wide.region_7.9_spmd.sunk | while | flops 716802 | bytes 573629 | solution.py:157
  147.9 29.2 %while.91 = (s32[]{:T(128)}, f32[5,16,128]{2,1,0:T(8,128)S(1)}, f32[5,5,16,128]{3,2,1,0:T(8,128)S(1)}, f32[16,5,16,128]{3,2,1,0:T(8,128)S(1)}, f32[16,5,5,16,128...) while((s32[]{:T(128)}, f32[5,16,128]{2,1,0:T(8,128)S(1)}, ...), condition=%wide.region_13.14_spmd.clone, body=%wide.region_10.13_spmd.clone.sunk | while | flops 4311044 | bytes 2703683 | solution.py:171
  178.7 9.3 %reduce.2 = f32[2048,30]{1,0:T(8,128)S(1)} reduce(f32[2048,1,30]{2,1,0:T(1,128)S(1)} %bitcast.222, f32[]{:T(128)} %broadcast.68), dimensions={1}, to_apply=%bitcast.172.reduce_sub_computation | reduce | bytes 491524
  189.8 3.4 %all-to-all-start.2 = ((f32[8,1,7680]{2,1,0:T(1,128)}), f32[8,1,7680]{2,1,0:T(1,128)S(1)}, u32[]{:S(2)}, u32[]{:S(2)}) async-start(f32[8,1,7680]{2,1,0:T(1,128)} %reshape.89), calls=%async_computation.2 | async-start | bytes 491520 | tf_op jit(solution)/shard_map/all_to_all | solution.py:101
  193.2 8.0 %all-to-all-done.2 = f32[8,1,7680]{2,1,0:T(1,128)S(1)} async-done(((f32[8,1,7680]{2,1,0:T(1,128)}), f32[8,1,7680]{2,1,0:T(1,128)S(1)}, u32[]{:S(2)}, u32[]{:S(2)}) %all-to-all-start.2) | async-done | bytes 245792 | tf_op jit(solution)/shard_map/all_to_all | solution.py:101
  205.3 5.6 %while.92 = (s32[]{:T(128)}, f32[5,256]{1,0:T(8,128)S(1)}, f32[8,5,256]{2,1,0:T(8,128)}, f32[8,5,5,256]{3,0,2,1:T(8,128)S(1)}, f32[8,5,256]{2,0,1:T(8,128)S(1)}, /*index=5*/s32[]{:T(128)}, s32[]{:T(128)}, s32[]{:T(128)}) while((s32[]{:T(128)}, f32[5,256]{1,0:T(8,128)S(1)}, f32[8,5,256]{2,1,0:T(8,128)}, ...), condition=%wide.region_16.17_spmd.clone, body=%wide.region_14.16_spmd.clone.sunk | while | flops 14084 | bytes 131191 | solution.py:87
  211.0 3.4 %all-to-all-start.3 = ((f32[8,5,256]{2,1,0:T(8,128)}), f32[8,5,256]{2,1,0:T(8,128)S(1)}, u32[]{:S(2)}, u32[]{:S(2)}) async-start(f32[8,5,256]{2,1,0:T(8,128)} %get-tuple-element.448), calls=%async_computation.3 | async-start | bytes 131072 | tf_op jit(solution)/shard_map/all_to_all | solution.py:105
  215.3 5.9 %all-to-all-done.3 = f32[8,5,256]{2,1,0:T(8,128)S(1)} async-done(((f32[8,5,256]{2,1,0:T(8,128)}), f32[8,5,256]{2,1,0:T(8,128)S(1)}, u32[]{:S(2)}, u32[]{:S(2)}) %all-to-all-start.3) | async-done | bytes 40992 | tf_op jit(solution)/shard_map/all_to_all | solution.py:105
  221.3 44.0 %while.89 = (s32[]{:T(128)}, f32[5,16,128]{2,1,0:T(8,128)S(1)}, f32[16,5,16,128]{3,2,1,0:T(8,128)S(1)}, f32[16,5,16,128]{3,2,1,0:T(8,128)}, f32[16,5,5,16,128]{4...) while((s32[]{:T(128)}, f32[5,16,128]{2,1,0:T(8,128)S(1)}, ...), condition=%wide.region_19.20_spmd, body=%wide.region_17.19_spmd.sunk | while | flops 727043 | bytes 696529 | solution.py:175
  (584 shorter events, 169.7 us)
Async XLA Ops:
  0.6 8.8 %copy-start = (f32[5,5]{1,0:T(8,128)S(1)}, f32[5,5]{1,0:T(8,128)}, u32[]{:S(2)}) copy-start(f32[5,5]{1,0:T(8,128)} %param.30) | copy-start | bytes 304
  0.6 8.8 %copy-start.1 = (f32[16,5,16,128]{3,2,1,0:T(8,128)S(1)}, f32[16,5,16,128]{3,2,1,0:T(8,128)}, u32[]{:S(2)}) copy-start(f32[16,5,16,128]{3,2,1,0:T(8,128)} %param.23) | copy-start | bytes 1966084
  1.6 9.1 %copy-start.11 = (f32[16,16,128]{2,1,0:T(8,128)}, f32[16,16,128]{2,1,0:T(8,128)S(1)}, u32[]{:S(2)}) copy-start(f32[16,16,128]{2,1,0:T(8,128)S(1)} %convert_element_type.13) | copy-start | bytes 393220
  3.1 7.6 %copy-start.24 = (s32[16,16,128]{2,1,0:T(8,128)S(1)}, s32[16,16,128]{2,1,0:T(8,128)}, u32[]{:S(2)}) copy-start(s32[16,16,128]{2,1,0:T(8,128)} %param.27) | copy-start | bytes 393220
  3.1 8.4 %copy-start.26 = (f32[6,5,5]{2,0,1:T(8,128)S(1)}, f32[6,5,5]{2,0,1:T(8,128)}, u32[]{:S(2)}) copy-start(f32[6,5,5]{2,0,1:T(8,128)} %param.29) | copy-start | bytes 1804
  3.1 8.4 %copy-start.27 = (f32[5,5]{1,0:T(8,128)S(1)}, f32[5,5]{1,0:T(8,128)}, u32[]{:S(2)}) copy-start(f32[5,5]{1,0:T(8,128)} %param.28) | copy-start | bytes 304
  3.2 11.2 %collective-permute-start = (f32[1,5,16,128]{3,1,2,0:T(8,128)S(1)}, f32[1,5,16,128]{3,1,2,0:T(8,128)S(1)}, u32[]{:S(2)}, u32[]{:S(2)}) collective-permute-start(f32[1,5,16,128]{3,1,2,0:T(8,128)S(1)} %get-tuple-element.649), channel_id=1, source_target_pairs={{0,4},{4,8},{8,12},{12,16},{16,20},{20,24},{24,28},{1,5},{5,9},{9,... | collective-permute-start | bytes 122888 | tf_op jit(solution)/shard_map/ppermute | solution.py:12
  8.2 6.2 %collective-permute-start.1 = (f32[1,5,16,128]{3,1,2,0:T(8,128)S(1)}, f32[1,5,16,128]{3,1,2,0:T(8,128)S(1)}, u32[]{:S(2)}, u32[]{:S(2)}) collective-permute-start(f32[1,5,16,128]{3,1,2,0:T(8,128)S(1)} %get-tuple-element.650), channel_id=1, source_target_pairs={{4,0},{8,4},{12,8},{16,12},{20,16},{24,20},{28,24},{5,1},{9,5},{13... | collective-permute-start | bytes 122888 | tf_op jit(solution)/shard_map/ppermute | solution.py:15
  10.7 3.0 %copy-start.25 = (s32[16,16,128]{2,1,0:T(8,128)S(1)}, s32[16,16,128]{2,1,0:T(8,128)}, u32[]{:S(2)}) copy-start(s32[16,16,128]{2,1,0:T(8,128)} %param.26) | copy-start | bytes 393220
  14.4 9.7 %copy-start.6 = (f32[1,5,16,128]{3,1,2,0:T(8,128)}, f32[1,5,16,128]{3,1,2,0:T(8,128)S(1)}, u32[]{:S(2)}) copy-start(f32[1,5,16,128]{3,1,2,0:T(8,128)S(1)} %collective-permute-done.1) | copy-start | bytes 122884
  14.4 6.9 %collective-permute-start.2 = (f32[18,5,1,128]{3,1,2,0:T(8,128)S(1)}, f32[18,5,1,128]{3,1,2,0:T(8,128)S(1)}, u32[]{:S(2)}, u32[]{:S(2)}) collective-permute-start(f32[18,5,1,128]{3,1,2,0:T(8,128)S(1)} %get-tuple-element.647), channel_id=1, source_target_pairs={{0,2},{1,3},{4,6},{5,7},{8,10},{9,11},{12,14},{13,15},{16,18},{17,... | collective-permute-start | bytes 138248 | tf_op jit(solution)/shard_map/ppermute | solution.py:12
  17.9 6.2 %collective-permute-start.3 = (f32[18,5,1,128]{3,1,2,0:T(8,128)S(1)}, f32[18,5,1,128]{3,1,2,0:T(8,128)S(1)}, u32[]{:S(2)}, u32[]{:S(2)}) collective-permute-start(f32[18,5,1,128]{3,1,2,0:T(8,128)S(1)} %get-tuple-element.648), channel_id=1, source_target_pairs={{2,0},{3,1},{6,4},{7,5},{10,8},{11,9},{14,12},{15,13},{18,16},{19,... | collective-permute-start | bytes 138248 | tf_op jit(solution)/shard_map/ppermute | solution.py:15
  21.3 2.8 %copy-start.13 = (f32[18,5,1,128]{3,1,2,0:T(8,128)}, f32[18,5,1,128]{3,1,2,0:T(8,128)S(1)}, u32[]{:S(2)}) copy-start(f32[18,5,1,128]{3,1,2,0:T(8,128)S(1)} %collective-permute-done.2) | copy-start | bytes 138244
  28.9 9.9 %collective-permute-start.4 = (f32[18,5,18,1]{2,3,1,0:T(1,128)}, f32[18,5,18,1]{2,3,1,0:T(1,128)}, u32[]{:S(2)}, u32[]{:S(2)}) collective-permute-start(f32[18,5,18,1]{2,3,1,0:T(1,128)} %copy.197), channel_id=1, source_target_pairs={{0,1},{2,3},{4,5},{6,7},{8,9},{10,11},{12,13},{14,15},{16,17},{18,... | collective-permute-start | bytes 19448 | tf_op jit(solution)/shard_map/ppermute | solution.py:12
  32.1 9.6 %collective-permute-start.5 = (f32[18,5,18,1]{2,3,1,0:T(1,128)}, f32[18,5,18,1]{2,3,1,0:T(1,128)}, u32[]{:S(2)}, u32[]{:S(2)}) collective-permute-start(f32[18,5,18,1]{2,3,1,0:T(1,128)} %copy.200), channel_id=1, source_target_pairs={{1,0},{3,2},{5,4},{7,6},{9,8},{11,10},{13,12},{15,14},{17,16},{19,... | collective-permute-start | bytes 19448 | tf_op jit(solution)/shard_map/ppermute | solution.py:15
  33.6 3.1 %copy-start.7 = (f32[1,5,16,128]{3,1,2,0:T(8,128)S(1)}, f32[1,5,16,128]{3,1,2,0:T(8,128)}, u32[]{:S(2)}) copy-start(f32[1,5,16,128]{3,1,2,0:T(8,128)} %copy-done.6) | copy-start | bytes 122884
  33.6 3.1 %copy-start.14 = (f32[18,5,1,128]{3,1,2,0:T(8,128)S(1)}, f32[18,5,1,128]{3,1,2,0:T(8,128)}, u32[]{:S(2)}) copy-start(f32[18,5,1,128]{3,1,2,0:T(8,128)} %copy-done.13) | copy-start | bytes 138244
  33.6 3.1 %copy-start.23 = (pred[16,16,128]{2,1,0:T(8,128)(4,1)S(1)}, pred[16,16,128]{2,1,0:T(8,128)(4,1)}, u32[]{:S(2)}) copy-start(pred[16,16,128]{2,1,0:T(8,128)(4,1)} %get-tuple-element.653) | copy-start | bytes 98308
  43.4 4.3 %copy-start.10 = (f32[16,5,16,128]{3,2,1,0:T(8,128)S(1)}, f32[16,5,16,128]{3,2,1,0:T(8,128)}, u32[]{:S(2)}) copy-start(f32[16,5,16,128]{3,2,1,0:T(8,128)} %param.24) | copy-start | bytes 1966084
  91.2 16.6 %all-to-all-start = ((f32[8,1,7680]{2,1,0:T(1,128)}), f32[8,1,7680]{2,1,0:T(1,128)S(1)}, u32[]{:S(2)}, u32[]{:S(2)}) async-start(f32[8,1,7680]{2,1,0:T(1,128)} %reshape.87), calls=%async_computation | async-start | bytes 491520 | tf_op jit(solution)/shard_map/all_to_all | solution.py:92
  117.6 10.8 %all-to-all-start.1 = ((f32[8,5,256]{2,1,0:T(8,128)}), f32[8,5,256]{2,1,0:T(8,128)S(1)}, u32[]{:S(2)}, u32[]{:S(2)}) async-start(f32[8,5,256]{2,1,0:T(8,128)} %get-tuple-element.444), calls=%async_computation.1 | async-start | bytes 131072 | tf_op jit(solution)/shard_map/all_to_all | solution.py:96
  128.5 19.4 %copy-start.19 = (f32[5,5]{1,0:T(8,128)S(1)}, f32[5,5]{1,0:T(8,128)}, u32[]{:S(2)}) copy-start(f32[5,5]{1,0:T(8,128)} %param.33) | copy-start | bytes 304
  189.8 11.5 %all-to-all-start.2 = ((f32[8,1,7680]{2,1,0:T(1,128)}), f32[8,1,7680]{2,1,0:T(1,128)S(1)}, u32[]{:S(2)}, u32[]{:S(2)}) async-start(f32[8,1,7680]{2,1,0:T(1,128)} %reshape.89), calls=%async_computation.2 | async-start | bytes 491520 | tf_op jit(solution)/shard_map/all_to_all | solution.py:101
  211.0 10.2 %all-to-all-start.3 = ((f32[8,5,256]{2,1,0:T(8,128)}), f32[8,5,256]{2,1,0:T(8,128)S(1)}, u32[]{:S(2)}, u32[]{:S(2)}) async-start(f32[8,5,256]{2,1,0:T(8,128)} %get-tuple-element.448), calls=%async_computation.3 | async-start | bytes 131072 | tf_op jit(solution)/shard_map/all_to_all | solution.py:105
  (14 other events, 26.4 us)
where the time goes:
time: 271 us; the launch traced here: 266 us
  other arithmetic  125 us (46%)
  matrix products  42.5 us (16%)
  waiting for transfers between devices  33.3 us (12%)
  starting transfers between devices  32 us (12%)
  local copies, waits for them, and re-layouts  28.1 us (10%)
  loops' own time  3.88 us (1%)
    reduce_sum x64, other arithmetic, volume_operator(): return jnp.sum(blocks * vector[..., None, :, :, :], axis=-3)  61.3 us
    dot_general x72, matrix products, const_apply(): jnp.einsum('ab,...byz->...ayz', matrix, vector, precision=lax.Precision.H...  28.5 us
    unnamed x5, other arithmetic  18.6 us
    dot_general x32, matrix products, couple(): jnp.einsum('ab,bcyz->acyz', matrix, transfer, precision=lax.Precision.HIG...  14.1 us
    dynamic_update_slice x16, other arithmetic, on_device(): final, swept = lax.scan(forward, incoming, (diag_inverse, residual))  12.7 us
    sub x16, other arithmetic, backward(): value - volume_operator(blocks, const_apply(upper_neighbour_block, carry))  12.6 us
    unnamed x68, local copies, waits for them, and re-layouts  11.9 us
    ppermute x3, starting transfers between devices, with_halo(): lax.ppermute(lax.slice_in_dim(block, block.shape[dim] - width, None, axis...  10.3 us
  transfers between devices with their start and end apart: 10, of which 5 were waited for; matrix products, arithmetic and copies ran while one was open for 6% of the time, Pallas kernels for 0%

commit v1 on v0

--- a/solution.py
+++ b/solution.py
@@ -89,8 +89,14 @@
 
 
 def carry_east(transfer, offset):
-    spread = lax.all_to_all(
-        pack_maps(transfer, offset), "gx", split_axis=2, concat_axis=0, tiled=True
+    spread = jnp.concatenate(
+        lax.all_to_all(
+            jnp.stack(jnp.split(pack_maps(transfer, offset), lax.axis_size("gx"), axis=2)),
+            "gx",
+            0,
+            0,
+        ),
+        axis=0,
     )
     incoming = column_chain(spread, offset.shape[0], False)
     returned = lax.all_to_all(incoming, "gx", split_axis=0, concat_axis=2, tiled=True)

time: 271 us -> 260 us (0.959)
  other arithmetic: 125 us -> 115 us
    unnamed x5 -> x4, other arithmetic: 18.6 us -> 9.37 us
    unnamed x68 -> x73, local copies, waits for them, and re-layouts: 11.9 us -> 12.6 us
  transfers between devices with their start and end apart: 10 -> 10, of which waited for: 5 -> 5; matrix products, arithmetic and copies ran while one was open for 6% -> 7% of each run, Pallas kernels for 0% -> 0%
where the time goes in v1:
time: 260 us; the launch traced here: 256 us
  other arithmetic  115 us (44%)
  matrix products  42.5 us (16%)
  waiting for transfers between devices  33.3 us (13%)
  starting transfers between devices  32 us (12%)
  local copies, waits for them, and re-layouts  28.6 us (11%)
  loops' own time  3.66 us (1%)
    reduce_sum x64, other arithmetic, volume_operator(): return jnp.sum(blocks * vector[..., None, :, :, :], axis=-3)  61.3 us
    dot_general x72, matrix products, const_apply(): jnp.einsum('ab,...byz->...ayz', matrix, vector, precision=lax.Precision.H...  28.4 us
    dot_general x32, matrix products, couple(): jnp.einsum('ab,bcyz->acyz', matrix, transfer, precision=lax.Precision.HIG...  14.1 us
    dynamic_update_slice x16, other arithmetic, on_device(): final, swept = lax.scan(forward, incoming, (diag_inverse, residual))  12.7 us
    unnamed x73, local copies, waits for them, and re-layouts  12.6 us
    sub x16, other arithmetic, backward(): value - volume_operator(blocks, const_apply(upper_neighbour_block, carry))  12.6 us
    ppermute x3, starting transfers between devices, with_halo(): lax.ppermute(lax.slice_in_dim(block, block.shape[dim] - width, None, axis...  10.3 us
    all_to_all x1, waiting for transfers between devices, carry_east(): lax.all_to_all(jnp.stack(jnp.split(pack_maps(transfer, offset), lax.axis_...  9.68 us
  transfers between devices with their start and end apart: 10, of which 5 were waited for; matrix products, arithmetic and copies ran while one was open for 7% of the time, Pallas kernels for 0%

profile of v1, /device:TPU:0, one launch (start us, length us, event | category | flops | bytes accessed | tf_op | source)
XLA Modules:
  0.0 255.9 jit_solution(9902694316995722756)
XLA Ops:
  3.2 5.0 %collective-permute-start = (f32[1,5,16,128]{3,1,2,0:T(8,128)S(1)}, f32[1,5,16,128]{3,1,2,0:T(8,128)S(1)}, u32[]{:S(2)}, u32[]{:S(2)}) collective-permute-start(f32[1,5,16,128]{3,1,2,0:T(8,128)S(1)} %get-tuple-element.649), channel_id=1, source_target_pairs={{0,4},{4,8},{8,12},{12,16},{16,20},{20,24},{24,28},{1,5},{5,9},{9,... | collective-permute-start | bytes 122888 | tf_op jit(solution)/shard_map/ppermute | solution.py:12
  11.5 2.2 fusion.37
  14.5 3.4 %collective-permute-start.2 = (f32[18,5,1,128]{3,1,2,0:T(8,128)S(1)}, f32[18,5,1,128]{3,1,2,0:T(8,128)S(1)}, u32[]{:S(2)}, u32[]{:S(2)}) collective-permute-start(f32[18,5,1,128]{3,1,2,0:T(8,128)S(1)} %get-tuple-element.647), channel_id=1, source_target_pairs={{0,2},{1,3},{4,6},{5,7},{8,10},{9,11},{12,14},{13,15},{16,18},{17,... | collective-permute-start | bytes 138248 | tf_op jit(solution)/shard_map/ppermute | solution.py:12
  21.3 2.8 %collective-permute-done.3 = f32[18,5,1,128]{3,1,2,0:T(8,128)S(1)} collective-permute-done((f32[18,5,1,128]{3,1,2,0:T(8,128)S(1)}, f32[18,5,1,128]{3,1,2,0:T(8,128)S(1)}, u32[]{:S(2)}, u32[]{:S(2)}) %collective-permute-start.3) | collective-permute-done | bytes 46112 | tf_op jit(solution)/shard_map/ppermute | solution.py:15
  26.4 2.6 copy.207
  33.6 3.0 %convolution_select_fusion = f32[16,16,128,5]{2,3,1,0:T(8,128)} fusion(f32[16,16,128,5]{2,3,1,0:T(8,128)S(1)} %fusion.35, f32[18,5,1,128]{3,1,2,0:T(8,128)} %copy-done.16, f32[1,5,16,128]{3,1,2,0:T(8,128)} %copy-done.6, f32[16,5,16,128]{3,1,2,0:T(8,128)S(1)} %copy_multiply_fusion, f32[1,5,16,128]{3,1,2,0:T(8,128)S(1)} %collective-permute-done, ...), kind=kOutput, calls=%fused_computation.52 | convolution fusion | flops 10581760 | bytes 2126948 | tf_op jit(solution)/shard_map/ab,...byz->...ayz/dot_general | solution.py:21
  36.6 2.2 convolution_select_fusion.1
  38.8 2.8 %copy.208 = f32[18,5,18,1]{3,1,2,0:T(8,128)} copy(f32[18,5,18,1]{2,3,1,0:T(1,128)} %collective-permute-done.4) | data formatting | bytes 12960 | tf_op jit(solution)/shard_map/ppermute | solution.py:12
  43.4 2.6 %convolution_select_fusion.5 = f32[16,16,128,5]{2,3,1,0:T(8,128)S(1)} fusion(f32[16,16,128,5]{2,3,1,0:T(8,128)S(1)} %fusion.35, f32[18,5,18,1]{3,1,2,0:T(8,128)} %copy.208, f32[18,5,1,128]{3,1,2,0:T(8,128)} %copy-done.16, f32[18,5,1,128]{3,1,2,0:T(8,128)} %copy-done.13, f32[1,5,16,128]{3,1,2,0:T(8,128)} %copy-done.6, ...), kind=kOutput, calls=%fused_computation.57 | convolution fusion | flops 10813440 | bytes 2179508 | tf_op jit(solution)/shard_map/ab,...byz->...ayz/dot_general | solution.py:21
  50.1 28.4 %while.87 = (s32[]{:T(128)}, f32[5,16,128]{2,1,0:T(8,128)S(1)}, f32[5,5,16,128]{3,2,1,0:T(8,128)S(1)}, f32[16,5,5,16,128]{4,3,2,1,0:T(8,128)}, f32[16,5,16,128]{...) while((s32[]{:T(128)}, f32[5,16,128]{2,1,0:T(8,128)S(1)}, f32[5,5,16,128]{3,2,1,0:T(8,128)S(1)}, ...), condition=%wide.region_3.4_spmd, body=%wide.region_0.3_spmd.sunk | while | flops 4249602 | bytes 2130205 | solution.py:161
  83.8 7.0 %all-to-all-start = ((f32[8,1,30,256]{3,1,2,0:T(1,128)}), f32[8,1,30,256]{3,1,2,0:T(1,128)S(1)}, u32[]{:S(2)}, u32[]{:S(2)}) async-start(f32[8,1,30,256]{3,1,2,0:T(1,128)} %fusion.61), calls=%async_computation | async-start | bytes 491520 | tf_op jit(solution)/shard_map/all_to_all | solution.py:93
  90.8 9.7 %all-to-all-done = f32[8,1,30,256]{3,1,2,0:T(1,128)S(1)} async-done(((f32[8,1,30,256]{3,1,2,0:T(1,128)}), f32[8,1,30,256]{3,1,2,0:T(1,128)S(1)}, u32[]{:S(2)}, u32[]{:S(2)}) %all-to-all-start) | async-done | bytes 245792 | tf_op jit(solution)/shard_map/all_to_all | solution.py:93
  101.1 5.7 %while.90 = (s32[]{:T(128)}, f32[5,256]{1,0:T(8,128)S(1)}, f32[8,5,256]{2,1,0:T(8,128)}, f32[8,5,5,256]{3,0,2,1:T(8,128)S(1)}, f32[8,5,256]{2,0,1:T(8,128)S(1)}, /*index=5*/s32[]{:T(128)}, s32[]{:T(128)}) while((s32[]{:T(128)}, f32[5,256]{1,0:T(8,128)S(1)}, f32[8,5,256]{2,1,0:T(8,128)}, f32[8,5,5,256]{3,0,2,1:T(8,128)S(1)}, ...), condition=%wide.region_6.7_spmd.clone, body=%wide.region_4.6_spmd.clone.sunk | while | flops 14083 | bytes 131679 | solution.py:87
  106.8 3.9 %all-to-all-start.1 = ((f32[8,5,256]{2,1,0:T(8,128)}), f32[8,5,256]{2,1,0:T(8,128)S(1)}, u32[]{:S(2)}, u32[]{:S(2)}) async-start(f32[8,5,256]{2,1,0:T(8,128)} %get-tuple-element.444), calls=%async_computation.1 | async-start | bytes 131072 | tf_op jit(solution)/shard_map/all_to_all | solution.py:102
  110.7 6.9 %all-to-all-done.1 = f32[8,5,256]{2,1,0:T(8,128)S(1)} async-done(((f32[8,5,256]{2,1,0:T(8,128)}), f32[8,5,256]{2,1,0:T(8,128)S(1)}, u32[]{:S(2)}, u32[]{:S(2)}) %all-to-all-start.1) | async-done | bytes 40992 | tf_op jit(solution)/shard_map/all_to_all | solution.py:102
  117.7 19.3 %while.88 = (s32[]{:T(128)}, f32[5,16,128]{2,1,0:T(8,128)S(1)}, f32[16,5,16,128]{3,2,1,0:T(8,128)S(1)}, f32[16,5,5,16,128]{4,3,2,1,0:T(8,128)}, f32[16,5,16,128]...) while((s32[]{:T(128)}, f32[5,16,128]{2,1,0:T(8,128)S(1)}, f32[16,5,16,128]{3,2,1,0:T(8,128)S(1)}, ...), condition=%wide.region_9.10_spmd, body=%wide.region_7.9_spmd.sunk | while | flops 716802 | bytes 573629 | solution.py:163
  137.1 29.2 %while.91 = (s32[]{:T(128)}, f32[5,16,128]{2,1,0:T(8,128)S(1)}, f32[5,5,16,128]{3,2,1,0:T(8,128)S(1)}, f32[16,5,16,128]{3,2,1,0:T(8,128)S(1)}, f32[16,5,5,16,128...) while((s32[]{:T(128)}, f32[5,16,128]{2,1,0:T(8,128)S(1)}, ...), condition=%wide.region_13.14_spmd.clone, body=%wide.region_10.13_spmd.clone.sunk | while | flops 4311044 | bytes 2703683 | solution.py:177
  168.4 9.4 %reduce = f32[2048,30]{1,0:T(8,128)S(1)} reduce(f32[2048,1,30]{2,1,0:T(1,128)S(1)} %bitcast.261, f32[]{:T(128)} %broadcast.68), dimensions={1}, to_apply=%bitcast.212.reduce_sub_computation | reduce | bytes 491524
  179.6 3.4 %all-to-all-start.2 = ((f32[8,1,7680]{2,1,0:T(1,128)}), f32[8,1,7680]{2,1,0:T(1,128)S(1)}, u32[]{:S(2)}, u32[]{:S(2)}) async-start(f32[8,1,7680]{2,1,0:T(1,128)} %reshape.91), calls=%async_computation.2 | async-start | bytes 491520 | tf_op jit(solution)/shard_map/all_to_all | solution.py:107
  183.0 8.0 %all-to-all-done.2 = f32[8,1,7680]{2,1,0:T(1,128)S(1)} async-done(((f32[8,1,7680]{2,1,0:T(1,128)}), f32[8,1,7680]{2,1,0:T(1,128)S(1)}, u32[]{:S(2)}, u32[]{:S(2)}) %all-to-all-start.2) | async-done | bytes 245792 | tf_op jit(solution)/shard_map/all_to_all | solution.py:107
  195.2 5.6 %while.92 = (s32[]{:T(128)}, f32[5,256]{1,0:T(8,128)S(1)}, f32[8,5,256]{2,1,0:T(8,128)}, f32[8,5,5,256]{3,0,2,1:T(8,128)S(1)}, f32[8,5,256]{2,0,1:T(8,128)S(1)}, /*index=5*/s32[]{:T(128)}, s32[]{:T(128)}, s32[]{:T(128)}) while((s32[]{:T(128)}, f32[5,256]{1,0:T(8,128)S(1)}, f32[8,5,256]{2,1,0:T(8,128)}, ...), condition=%wide.region_16.17_spmd.clone, body=%wide.region_14.16_spmd.clone.sunk | while | flops 14084 | bytes 131191 | solution.py:87
  200.8 3.4 %all-to-all-start.3 = ((f32[8,5,256]{2,1,0:T(8,128)}), f32[8,5,256]{2,1,0:T(8,128)S(1)}, u32[]{:S(2)}, u32[]{:S(2)}) async-start(f32[8,5,256]{2,1,0:T(8,128)} %get-tuple-element.448), calls=%async_computation.3 | async-start | bytes 131072 | tf_op jit(solution)/shard_map/all_to_all | solution.py:111
  205.1 5.9 %all-to-all-done.3 = f32[8,5,256]{2,1,0:T(8,128)S(1)} async-done(((f32[8,5,256]{2,1,0:T(8,128)}), f32[8,5,256]{2,1,0:T(8,128)S(1)}, u32[]{:S(2)}, u32[]{:S(2)}) %all-to-all-start.3) | async-done | bytes 40992 | tf_op jit(solution)/shard_map/all_to_all | solution.py:111
  211.1 44.0 %while.89 = (s32[]{:T(128)}, f32[5,16,128]{2,1,0:T(8,128)S(1)}, f32[16,5,16,128]{3,2,1,0:T(8,128)S(1)}, f32[16,5,16,128]{3,2,1,0:T(8,128)}, f32[16,5,5,16,128]{4...) while((s32[]{:T(128)}, f32[5,16,128]{2,1,0:T(8,128)S(1)}, ...), condition=%wide.region_19.20_spmd, body=%wide.region_17.19_spmd.sunk | while | flops 727043 | bytes 696529 | solution.py:181
  (588 shorter events, 166.9 us)
Async XLA Ops:
  0.6 8.8 %copy-start = (f32[5,5]{1,0:T(8,128)S(1)}, f32[5,5]{1,0:T(8,128)}, u32[]{:S(2)}) copy-start(f32[5,5]{1,0:T(8,128)} %param.30) | copy-start | bytes 304
  0.6 8.8 %copy-start.1 = (f32[16,5,16,128]{3,2,1,0:T(8,128)S(1)}, f32[16,5,16,128]{3,2,1,0:T(8,128)}, u32[]{:S(2)}) copy-start(f32[16,5,16,128]{3,2,1,0:T(8,128)} %param.23) | copy-start | bytes 1966084
  1.6 9.1 %copy-start.11 = (f32[16,16,128]{2,1,0:T(8,128)}, f32[16,16,128]{2,1,0:T(8,128)S(1)}, u32[]{:S(2)}) copy-start(f32[16,16,128]{2,1,0:T(8,128)S(1)} %convert_element_type.13) | copy-start | bytes 393220
  3.1 7.6 %copy-start.24 = (s32[16,16,128]{2,1,0:T(8,128)S(1)}, s32[16,16,128]{2,1,0:T(8,128)}, u32[]{:S(2)}) copy-start(s32[16,16,128]{2,1,0:T(8,128)} %param.27) | copy-start | bytes 393220
  3.1 8.4 %copy-start.26 = (f32[6,5,5]{2,0,1:T(8,128)S(1)}, f32[6,5,5]{2,0,1:T(8,128)}, u32[]{:S(2)}) copy-start(f32[6,5,5]{2,0,1:T(8,128)} %param.29) | copy-start | bytes 1804
  3.1 8.4 %copy-start.27 = (f32[5,5]{1,0:T(8,128)S(1)}, f32[5,5]{1,0:T(8,128)}, u32[]{:S(2)}) copy-start(f32[5,5]{1,0:T(8,128)} %param.28) | copy-start | bytes 304
  3.2 11.3 %collective-permute-start = (f32[1,5,16,128]{3,1,2,0:T(8,128)S(1)}, f32[1,5,16,128]{3,1,2,0:T(8,128)S(1)}, u32[]{:S(2)}, u32[]{:S(2)}) collective-permute-start(f32[1,5,16,128]{3,1,2,0:T(8,128)S(1)} %get-tuple-element.649), channel_id=1, source_target_pairs={{0,4},{4,8},{8,12},{12,16},{16,20},{20,24},{24,28},{1,5},{5,9},{9,... | collective-permute-start | bytes 122888 | tf_op jit(solution)/shard_map/ppermute | solution.py:12
  8.2 6.2 %collective-permute-start.1 = (f32[1,5,16,128]{3,1,2,0:T(8,128)S(1)}, f32[1,5,16,128]{3,1,2,0:T(8,128)S(1)}, u32[]{:S(2)}, u32[]{:S(2)}) collective-permute-start(f32[1,5,16,128]{3,1,2,0:T(8,128)S(1)} %get-tuple-element.650), channel_id=1, source_target_pairs={{4,0},{8,4},{12,8},{16,12},{20,16},{24,20},{28,24},{5,1},{9,5},{13... | collective-permute-start | bytes 122888 | tf_op jit(solution)/shard_map/ppermute | solution.py:15
  10.7 3.0 %copy-start.25 = (s32[16,16,128]{2,1,0:T(8,128)S(1)}, s32[16,16,128]{2,1,0:T(8,128)}, u32[]{:S(2)}) copy-start(s32[16,16,128]{2,1,0:T(8,128)} %param.26) | copy-start | bytes 393220
  14.4 9.7 %copy-start.6 = (f32[1,5,16,128]{3,1,2,0:T(8,128)}, f32[1,5,16,128]{3,1,2,0:T(8,128)S(1)}, u32[]{:S(2)}) copy-start(f32[1,5,16,128]{3,1,2,0:T(8,128)S(1)} %collective-permute-done.1) | copy-start | bytes 122884
  14.5 6.9 %collective-permute-start.2 = (f32[18,5,1,128]{3,1,2,0:T(8,128)S(1)}, f32[18,5,1,128]{3,1,2,0:T(8,128)S(1)}, u32[]{:S(2)}, u32[]{:S(2)}) collective-permute-start(f32[18,5,1,128]{3,1,2,0:T(8,128)S(1)} %get-tuple-element.647), channel_id=1, source_target_pairs={{0,2},{1,3},{4,6},{5,7},{8,10},{9,11},{12,14},{13,15},{16,18},{17,... | collective-permute-start | bytes 138248 | tf_op jit(solution)/shard_map/ppermute | solution.py:12
  17.9 6.2 %collective-permute-start.3 = (f32[18,5,1,128]{3,1,2,0:T(8,128)S(1)}, f32[18,5,1,128]{3,1,2,0:T(8,128)S(1)}, u32[]{:S(2)}, u32[]{:S(2)}) collective-permute-start(f32[18,5,1,128]{3,1,2,0:T(8,128)S(1)} %get-tuple-element.648), channel_id=1, source_target_pairs={{2,0},{3,1},{6,4},{7,5},{10,8},{11,9},{14,12},{15,13},{18,16},{19,... | collective-permute-start | bytes 138248 | tf_op jit(solution)/shard_map/ppermute | solution.py:15
  21.3 2.8 %copy-start.13 = (f32[18,5,1,128]{3,1,2,0:T(8,128)}, f32[18,5,1,128]{3,1,2,0:T(8,128)S(1)}, u32[]{:S(2)}) copy-start(f32[18,5,1,128]{3,1,2,0:T(8,128)S(1)} %collective-permute-done.2) | copy-start | bytes 138244
  28.9 9.9 %collective-permute-start.4 = (f32[18,5,18,1]{2,3,1,0:T(1,128)}, f32[18,5,18,1]{2,3,1,0:T(1,128)}, u32[]{:S(2)}, u32[]{:S(2)}) collective-permute-start(f32[18,5,18,1]{2,3,1,0:T(1,128)} %copy.207), channel_id=1, source_target_pairs={{0,1},{2,3},{4,5},{6,7},{8,9},{10,11},{12,13},{14,15},{16,17},{18,... | collective-permute-start | bytes 19448 | tf_op jit(solution)/shard_map/ppermute | solution.py:12
  32.1 9.5 %collective-permute-start.5 = (f32[18,5,18,1]{2,3,1,0:T(1,128)}, f32[18,5,18,1]{2,3,1,0:T(1,128)}, u32[]{:S(2)}, u32[]{:S(2)}) collective-permute-start(f32[18,5,18,1]{2,3,1,0:T(1,128)} %copy.210), channel_id=1, source_target_pairs={{1,0},{3,2},{5,4},{7,6},{9,8},{11,10},{13,12},{15,14},{17,16},{19,... | collective-permute-start | bytes 19448 | tf_op jit(solution)/shard_map/ppermute | solution.py:15
  33.6 3.1 %copy-start.7 = (f32[1,5,16,128]{3,1,2,0:T(8,128)S(1)}, f32[1,5,16,128]{3,1,2,0:T(8,128)}, u32[]{:S(2)}) copy-start(f32[1,5,16,128]{3,1,2,0:T(8,128)} %copy-done.6) | copy-start | bytes 122884
  33.6 3.1 %copy-start.14 = (f32[18,5,1,128]{3,1,2,0:T(8,128)S(1)}, f32[18,5,1,128]{3,1,2,0:T(8,128)}, u32[]{:S(2)}) copy-start(f32[18,5,1,128]{3,1,2,0:T(8,128)} %copy-done.13) | copy-start | bytes 138244
  33.6 3.1 %copy-start.23 = (pred[16,16,128]{2,1,0:T(8,128)(4,1)S(1)}, pred[16,16,128]{2,1,0:T(8,128)(4,1)}, u32[]{:S(2)}) copy-start(pred[16,16,128]{2,1,0:T(8,128)(4,1)} %get-tuple-element.653) | copy-start | bytes 98308
  43.4 4.3 %copy-start.10 = (f32[16,5,16,128]{3,2,1,0:T(8,128)S(1)}, f32[16,5,16,128]{3,2,1,0:T(8,128)}, u32[]{:S(2)}) copy-start(f32[16,5,16,128]{3,2,1,0:T(8,128)} %param.24) | copy-start | bytes 1966084
  83.8 16.6 %all-to-all-start = ((f32[8,1,30,256]{3,1,2,0:T(1,128)}), f32[8,1,30,256]{3,1,2,0:T(1,128)S(1)}, u32[]{:S(2)}, u32[]{:S(2)}) async-start(f32[8,1,30,256]{3,1,2,0:T(1,128)} %fusion.61), calls=%async_computation | async-start | bytes 491520 | tf_op jit(solution)/shard_map/all_to_all | solution.py:93
  106.8 10.8 %all-to-all-start.1 = ((f32[8,5,256]{2,1,0:T(8,128)}), f32[8,5,256]{2,1,0:T(8,128)S(1)}, u32[]{:S(2)}, u32[]{:S(2)}) async-start(f32[8,5,256]{2,1,0:T(8,128)} %get-tuple-element.444), calls=%async_computation.1 | async-start | bytes 131072 | tf_op jit(solution)/shard_map/all_to_all | solution.py:102
  117.7 19.4 %copy-start.19 = (f32[5,5]{1,0:T(8,128)S(1)}, f32[5,5]{1,0:T(8,128)}, u32[]{:S(2)}) copy-start(f32[5,5]{1,0:T(8,128)} %param.33) | copy-start | bytes 304
  179.6 11.5 %all-to-all-start.2 = ((f32[8,1,7680]{2,1,0:T(1,128)}), f32[8,1,7680]{2,1,0:T(1,128)S(1)}, u32[]{:S(2)}, u32[]{:S(2)}) async-start(f32[8,1,7680]{2,1,0:T(1,128)} %reshape.91), calls=%async_computation.2 | async-start | bytes 491520 | tf_op jit(solution)/shard_map/all_to_all | solution.py:107
  200.8 10.2 %all-to-all-start.3 = ((f32[8,5,256]{2,1,0:T(8,128)}), f32[8,5,256]{2,1,0:T(8,128)S(1)}, u32[]{:S(2)}, u32[]{:S(2)}) async-start(f32[8,5,256]{2,1,0:T(8,128)} %get-tuple-element.448), calls=%async_computation.3 | async-start | bytes 131072 | tf_op jit(solution)/shard_map/all_to_all | solution.py:111
  (14 other events, 26.4 us)
